TPU v7x, 128 devices: a whole 4x4x4 slice. The times are simulated.
128 devices in a mesh: vel: 8 (over y, z_lo), space: 16 (over x, z_hi, core).
Axes of the slice: x: 4, y: 4, z: 4 (z_hi: 2, z_lo: 2; z = z_hi * 2 + z_lo), core: 2. Of those that a mesh axis runs over, the one named last changes fastest.
Arguments:
- density: float32 [1024, 64, 8, 128], P('vel', 'space'), may hold values from -6 to 6
- limiter: int32 [64, 8, 128], P('space'), may hold values from 0 to 2
- heading: int32 [1024], P('vel'), may hold values from 0 to 1
- courant: float32 [1024], P('vel'), may hold values from 0.1 to 0.9
- kernel_slices: bfloat16 [16, 1024, 1024], P('space', None, 'vel'), may hold values from -0.046875 to 0.046875
Outputs:
- transported: float32 [1024, 64, 8, 128], P('vel', 'space')
- collision: float32 [1024, 64, 8, 128], P('vel', 'space')
Inputs may be any that keep to these rules, and one draw needn't show every extreme that they name: `limiter`: 0 no slope, 1 minmod slope, 2 central slope.
All inputs are finite; a program needn't handle non-finite values.
Results may differ from a plain program's by a relative error of at most 0.0041.
Values may be sent and summed in bfloat16 or wider, within the bound.
No kernel may reach another device: no remote copies, remote signals or barrier semaphores. Data moves between devices by JAX's collectives and lax.ppermute only.
A program may use at most 128 MiB of HBM per device.

v0:
```python
import jax
import jax.numpy as jnp
from jax import lax
from jax.sharding import PartitionSpec as P

V = 1024
SLICES = 16


def extended(shard, sides, width):
    for axis, dim in sides:
        size, length = (lax.axis_size(axis), shard.shape[dim])
        up = [(i, (i + 1) % size) for i in range(size - 1)]
        down = [(j, i) for i, j in up]
        last = lax.slice_in_dim(shard, length - width, length, axis=dim)
        first = lax.slice_in_dim(shard, 0, width, axis=dim)
        before = lax.ppermute(last, axis, up)
        after = lax.ppermute(first, axis, down)
        shard = jnp.concatenate([before, shard, after], axis=dim)
    return shard


def limited_slopes(left_diff, right_diff, limiter):
    minmod_slope = jnp.where(
        left_diff * right_diff > 0,
        jnp.sign(left_diff) * jnp.minimum(jnp.abs(left_diff), jnp.abs(right_diff)),
        jnp.zeros_like(left_diff),
    )
    central = 0.5 * (left_diff + right_diff)
    codes = limiter[None]
    return jnp.where(
        codes == 1, minmod_slope, jnp.where(codes == 2, central, jnp.zeros_like(central))
    )


def make_fold(source, totals, pieces):
    stride = V // SLICES

    def one_slice(counter, running):
        matrix = lax.dynamic_index_in_dim(pieces, counter, 0, keepdims=False)
        projected = lax.dot_general(
            matrix, source, (((0,), (0,)), ((), ())), preferred_element_type=jnp.float32
        )
        weight = lax.dynamic_index_in_dim(source, counter * stride, 0, keepdims=True).astype(
            jnp.float32
        )
        return running + weight * projected

    return lax.fori_loop(0, pieces.shape[0], one_slice, totals)


def local(density, limiter, heading, courant, kernel_slices):
    padded = extended(density, (("space", 1),), 1)
    left_diff = density - padded[:, :-2]
    right_diff = padded[:, 2:] - density
    slopes = limited_slopes(left_diff, right_diff, limiter)
    upwind = (2 * heading - 1).astype(jnp.float32)[:, None, None, None]
    rebuilt = density + 0.5 * upwind * slopes
    rebuilt_pad = extended(rebuilt, (("space", 1),), 1)
    forward = (heading == 1)[:, None, None, None]
    upstream = jnp.where(forward, rebuilt_pad[:, :-2], rebuilt_pad[:, 2:])
    transported = density - courant[:, None, None, None] * (rebuilt - upstream)
    flattened = transported.astype(jnp.bfloat16).reshape(density.shape[0], -1)
    columns = lax.all_to_all(flattened, "vel", split_axis=1, concat_axis=0, tiled=True)
    full_slices = lax.all_gather(kernel_slices, "vel", axis=2, tiled=True)
    initial = jnp.zeros(columns.shape, jnp.float32)
    summed = make_fold(columns, initial, lax.all_gather(full_slices, "space", axis=0, tiled=True))
    restored = lax.all_to_all(summed, "vel", split_axis=0, concat_axis=1, tiled=True)
    return (transported, restored.reshape(density.shape))


def solution(mesh):
    return jax.shard_map(
        local,
        mesh=mesh,
        in_specs=(
            P("vel", "space", None, None),
            P("space", None, None),
            P("vel"),
            P("vel"),
            P("space", None, "vel"),
        ),
        out_specs=(P("vel", "space", None, None), P("vel", "space", None, None)),
        check_vma=False,
    )
```

profile of v0, /device:TPU:1, one launch (start us, length us, event | category | flops | bytes accessed | tf_op | source)
XLA Modules:
  0.0 379.8 jit_solution(10808552207556664224)
XLA Ops:
  7.2 0.0 all-gather.3.cloned.1.call-start
  7.2 0.7 all-gather.3.cloned.1.call-update
  7.9 0.0 all-gather.5.cloned.1.call-start
  7.9 61.5 %all-gather.3.cloned.1.call-done = bf16[1,1024,1024]{2,1,0:T(8,128)(2,1)} async-done(((bf16[1,1024,128]{2,1,0:T(8,128)(2,1)}), bf16[1,1024,1024]{2,1,0:T(8,128)(2,1)}) %all-gather.3.cloned.1.call-update) | async-done | bytes 2097168 | tf_op jit(solution)/shard_map/all_gather | solution.py:65
  69.5 0.0 all-gather.5.cloned.1.call-update
  69.5 2.0 copy.16
  71.5 0.0 copy-start.4
  71.5 0.0 copy-start.2
  71.5 0.1 fusion.18
  71.6 6.6 %collective-permute-start = (f32[128,1,8,128]{0,3,2,1:T(8,128)S(1)}, f32[128,1,8,128]{0,3,2,1:T(8,128)S(1)}, u32[]{:S(2)}, u32[]{:S(2)}) collective-permute-start(f32[128,1,8,128]{0,3,2,1:T(8,128)S(1)} %get-tuple-element.111), channel_id=1, source_target_pairs={{0,1},{1,2},{2,3},{3,4},{4,5},{5,6},{6,7},{7,8},{8,9},{9,10},{10,1... | collective-permute-start | bytes 1572872 | tf_op jit(solution)/shard_map/ppermute | solution.py:17
  78.2 1.9 collective-permute-start.1
  80.2 11.6 %collective-permute-done = f32[128,1,8,128]{0,3,2,1:T(8,128)S(1)} collective-permute-done((f32[128,1,8,128]{0,3,2,1:T(8,128)S(1)}, f32[128,1,8,128]{0,3,2,1:T(8,128)S(1)}, u32[]{:S(2)}, u32[]{:S(2)}) %collective-permute-start) | collective-permute-done | bytes 524320 | tf_op jit(solution)/shard_map/ppermute | solution.py:17
  91.8 0.0 collective-permute-done.1
  91.8 1.9 multiply_add_fusion
  93.7 0.0 copy-start.3
  93.7 0.1 fusion.17
  93.8 5.9 %collective-permute-start.2 = (f32[128,1,8,128]{0,3,2,1:T(8,128)S(1)}, f32[128,1,8,128]{0,3,2,1:T(8,128)S(1)}, u32[]{:S(2)}, u32[]{:S(2)}) collective-permute-start(f32[128,1,8,128]{0,3,2,1:T(8,128)S(1)} %get-tuple-element.109), channel_id=1, source_target_pairs={{0,1},{1,2},{2,3},{3,4},{4,5},{5,6},{6,7},{7,8},{8,9},{9,10},{10,1... | collective-permute-start | bytes 1572872 | tf_op jit(solution)/shard_map/ppermute | solution.py:17
  99.7 1.9 collective-permute-start.3
  101.6 26.6 %collective-permute-done.2 = f32[128,1,8,128]{0,3,2,1:T(8,128)S(1)} collective-permute-done((f32[128,1,8,128]{0,3,2,1:T(8,128)S(1)}, f32[128,1,8,128]{0,3,2,1:T(8,128)S(1)}, u32[]{:S(2)}, u32[]{:S(2)}) %collective-permute-start.2) | collective-permute-done | bytes 524320 | tf_op jit(solution)/shard_map/ppermute | solution.py:17
  128.2 0.0 collective-permute-done.3
  128.2 1.9 fusion.15
  130.1 1.3 copy.17
  131.4 3.6 all-to-all-start
  135.0 10.2 %all-to-all-done = bf16[128,8,512]{2,0,1:T(8,128)(2,1)S(1)} async-done(((bf16[128,8,512]{2,0,1:T(8,128)(2,1)}), bf16[128,8,512]{2,0,1:T(8,128)(2,1)S(1)}, u32[]{:S(2)}, u32[]{:S(2)}) %all-to-all-start) | async-done | bytes 1048608 | tf_op jit(solution)/shard_map/all_to_all | solution.py:64
  145.2 135.5 %all-gather.5.cloned.1.call-done = bf16[16,1024,1024]{2,1,0:T(8,128)(2,1)} async-done(((bf16[1,1024,1024]{2,1,0:T(8,128)(2,1)}), bf16[16,1024,1024]{2,1,0:T(8,128)(2,1)}) %all-gather.5.cloned.1.call-update) | async-done | bytes 33554448 | tf_op jit(solution)/shard_map/all_gather | solution.py:67
  280.7 51.4 %while.14 = (s32[]{:T(128)}, f32[1024,512]{1,0:T(8,128)S(1)}, bf16[1024,512]{1,0:T(8,128)(2,1)S(1)}, bf16[16,1024,1024]{2,1,0:T(8,128)(2,1)}, s32[]{:T(128)}, /*index=5*/s32[]{:T(128)}, s32[]{:T(128)}, s32[]{:T(128)}) while((s32[]{:T(128)}, f32[1024,512]{1,0:T(8,128)S(1)}, bf16[1024,512]{1,0:T(8,128)(2,1)S(1)}, ...), condition=%wide.region_1.2_spmd.clone, body=%wide.region_0.1_spmd.clone.sunk | while | flops 1075315200 | bytes 7345809 | solution.py:49
  280.7 3.2 select_add_fusion.2
  283.9 3.2 select_add_fusion.2
  287.1 3.2 select_add_fusion.2
  290.4 3.2 select_add_fusion.2
  293.6 3.2 select_add_fusion.2
  296.8 3.2 select_add_fusion.2
  300.0 3.2 select_add_fusion.2
  303.2 3.2 select_add_fusion.2
  306.4 3.2 select_add_fusion.2
  309.7 3.2 select_add_fusion.2
  312.9 3.2 select_add_fusion.2
  316.1 3.2 select_add_fusion.2
  319.3 3.2 select_add_fusion.2
  322.5 3.2 select_add_fusion.2
  325.7 3.2 select_add_fusion.2
  329.0 3.2 select_add_fusion.2
  332.2 1.3 copy-done.1
  333.4 4.5 %all-to-all-start.1 = ((f32[8,128,512]{2,1,0:T(8,128)}), f32[8,128,512]{2,1,0:T(8,128)}, u32[]{:S(2)}, u32[]{:S(2)}) async-start(f32[8,128,512]{2,1,0:T(8,128)} %bitcast.23), calls=%async_computation.1 | async-start | bytes 4194304 | tf_op jit(solution)/shard_map/all_to_all | solution.py:68
  337.9 2.0 copy.19
  339.9 29.2 %all-to-all-done.1 = f32[8,128,512]{2,1,0:T(8,128)} async-done(((f32[8,128,512]{2,1,0:T(8,128)}), f32[8,128,512]{2,1,0:T(8,128)}, u32[]{:S(2)}, u32[]{:S(2)}) %all-to-all-start.1) | async-done | bytes 2097184 | tf_op jit(solution)/shard_map/all_to_all | solution.py:68
  369.1 1.9 copy.18
  371.0 2.0 copy.20
  (26 shorter events, 0.2 us)
Async XLA Ops:
  7.2 62.3 %all-gather.3.cloned.1.call-start = ((), (), s32[]{:S(2)}) async-start(), calls=%async_computation.2 | async-start | bytes 2359296 | tf_op jit(solution)/shard_map/all_gather | solution.py:65
  7.9 272.8 %all-gather.5.cloned.1.call-start = ((), (), s32[]{:S(2)}) async-start(), calls=%async_computation.3 | async-start | bytes 35651584 | tf_op jit(solution)/shard_map/all_gather | solution.py:67
  71.5 8.6 %copy-start.4 = (s32[128]{0:T(128)S(1)}, s32[128]{0:T(128)}, u32[]{:S(2)}) copy-start(s32[128]{0:T(128)} %param.9) | copy-start | bytes 1540
  71.5 8.7 %copy-start.2 = (s32[4,8,128]{2,1,0:T(8,128)S(1)}, s32[4,8,128]{2,1,0:T(8,128)}, u32[]{:S(2)}) copy-start(s32[4,8,128]{2,1,0:T(8,128)} %param.8) | copy-start | bytes 49156
  71.6 20.2 %collective-permute-start = (f32[128,1,8,128]{0,3,2,1:T(8,128)S(1)}, f32[128,1,8,128]{0,3,2,1:T(8,128)S(1)}, u32[]{:S(2)}, u32[]{:S(2)}) collective-permute-start(f32[128,1,8,128]{0,3,2,1:T(8,128)S(1)} %get-tuple-element.111), channel_id=1, source_target_pairs={{0,1},{1,2},{2,3},{3,4},{4,5},{5,6},{6,7},{7,8},{8,9},{9,10},{10,1... | collective-permute-start | bytes 1572872 | tf_op jit(solution)/shard_map/ppermute | solution.py:17
  78.2 13.6 %collective-permute-start.1 = (f32[128,1,8,128]{0,3,2,1:T(8,128)S(1)}, f32[128,1,8,128]{0,3,2,1:T(8,128)S(1)}, u32[]{:S(2)}, u32[]{:S(2)}) collective-permute-start(f32[128,1,8,128]{0,3,2,1:T(8,128)S(1)} %get-tuple-element.112), channel_id=1, source_target_pairs={{1,0},{2,1},{3,2},{4,3},{5,4},{6,5},{7,6},{8,7},{9,8},{10,9},{11,1... | collective-permute-start | bytes 1572872 | tf_op jit(solution)/shard_map/ppermute | solution.py:18
  93.7 34.5 %copy-start.3 = (f32[128]{0:T(128)S(1)}, f32[128]{0:T(128)}, u32[]{:S(2)}) copy-start(f32[128]{0:T(128)} %param.10) | copy-start | bytes 1540
  93.8 34.4 %collective-permute-start.2 = (f32[128,1,8,128]{0,3,2,1:T(8,128)S(1)}, f32[128,1,8,128]{0,3,2,1:T(8,128)S(1)}, u32[]{:S(2)}, u32[]{:S(2)}) collective-permute-start(f32[128,1,8,128]{0,3,2,1:T(8,128)S(1)} %get-tuple-element.109), channel_id=1, source_target_pairs={{0,1},{1,2},{2,3},{3,4},{4,5},{5,6},{6,7},{7,8},{8,9},{9,10},{10,1... | collective-permute-start | bytes 1572872 | tf_op jit(solution)/shard_map/ppermute | solution.py:17
  99.7 28.5 %collective-permute-start.3 = (f32[128,1,8,128]{0,3,2,1:T(8,128)S(1)}, f32[128,1,8,128]{0,3,2,1:T(8,128)S(1)}, u32[]{:S(2)}, u32[]{:S(2)}) collective-permute-start(f32[128,1,8,128]{0,3,2,1:T(8,128)S(1)} %get-tuple-element.110), channel_id=1, source_target_pairs={{1,0},{2,1},{3,2},{4,3},{5,4},{6,5},{7,6},{8,7},{9,8},{10,9},{11,1... | collective-permute-start | bytes 1572872 | tf_op jit(solution)/shard_map/ppermute | solution.py:18
  131.4 13.8 %all-to-all-start = ((bf16[128,8,512]{2,0,1:T(8,128)(2,1)}), bf16[128,8,512]{2,0,1:T(8,128)(2,1)S(1)}, u32[]{:S(2)}, u32[]{:S(2)}) async-start(bf16[128,8,512]{2,0,1:T(8,128)(2,1)} %copy.17), calls=%async_computation | async-start | bytes 2097152 | tf_op jit(solution)/shard_map/all_to_all | solution.py:64
  332.1 1.3 copy-start.1
  333.4 4.5 %copy-start = (f32[128,4,8,128]{0,3,2,1:T(8,128)S(1)}, f32[128,4,8,128]{0,3,2,1:T(8,128)}, u32[]{:S(2)}) copy-start(f32[128,4,8,128]{0,3,2,1:T(8,128)} %get-tuple-element.108) | copy-start | bytes 6291460
  333.4 35.7 %all-to-all-start.1 = ((f32[8,128,512]{2,1,0:T(8,128)}), f32[8,128,512]{2,1,0:T(8,128)}, u32[]{:S(2)}, u32[]{:S(2)}) async-start(f32[8,128,512]{2,1,0:T(8,128)} %bitcast.23), calls=%async_computation.1 | async-start | bytes 4194304 | tf_op jit(solution)/shard_map/all_to_all | solution.py:68
Sparse Core Ops, SparseCore 0:
  9.6 59.8 all-gather.2
  71.8 208.8 all-gather.4
where the time goes:
time: 381 us; the launch traced here: 380 us
  waiting for transfers between devices  275 us (72%)
  matrix products  50.7 us (13%)
  starting transfers between devices  24.5 us (6%)
  between operations  14.2 us (4%)
  local copies, waits for them, and re-layouts  10.6 us (3%)
  other arithmetic  3.97 us (1%)
    all_gather x1, waiting for transfers between devices, local(): lax.all_gather(full_slices, 'space', axis=0, tiled=True)  136 us
    all_gather x1, waiting for transfers between devices, local(): full_slices = lax.all_gather(kernel_slices, 'vel', axis=2, tiled=True)  61.5 us
    dot_general x16, matrix products, one_slice(): lax.dot_general(matrix, source, (((0,), (0,)), ((), ())), preferred_eleme...  50.7 us
    ppermute x2, waiting for transfers between devices, extended(): before = lax.ppermute(last, axis, up)  38.2 us
    all_to_all x1, waiting for transfers between devices, local(): lax.all_to_all(summed, 'vel', split_axis=0, concat_axis=1, tiled=True)  29.2 us
    ppermute x2, starting transfers between devices, extended(): before = lax.ppermute(last, axis, up)  12.5 us
    all_to_all x1, waiting for transfers between devices, local(): lax.all_to_all(flattened, 'vel', split_axis=1, concat_axis=0, tiled=True)  10.2 us
  transfers between devices with their start and end apart: 8, of which 6 were waited for; matrix products, arithmetic and copies ran while one was open for 2% of the time, Pallas kernels for 0%

commit v1 on v0

--- a/solution.py
+++ b/solution.py
@@ -62,7 +62,8 @@
     transported = density - courant[:, None, None, None] * (rebuilt - upstream)
     flattened = transported.astype(jnp.bfloat16).reshape(density.shape[0], -1)
     columns = lax.all_to_all(flattened, "vel", split_axis=1, concat_axis=0, tiled=True)
-    full_slices = lax.all_gather(kernel_slices, "vel", axis=2, tiled=True)
+    sent = jnp.stack([kernel_slices] * lax.axis_size("vel"))
+    full_slices = jnp.concatenate(lax.all_to_all(sent, "vel", 0, 0), axis=2)
     initial = jnp.zeros(columns.shape, jnp.float32)
     summed = make_fold(columns, initial, lax.all_gather(full_slices, "space", axis=0, tiled=True))
     restored = lax.all_to_all(summed, "vel", split_axis=0, concat_axis=1, tiled=True)

time: 381 us -> 357 us (0.937)
  waiting for transfers between devices: 275 us -> 215 us
  blocking collectives: 0 us -> 31.9 us
  local copies, waits for them, and re-layouts: 10.6 us -> 18.4 us
    all_gather x1 -> x0, waiting for transfers between devices: 61.5 us -> none  [local(): full_slices = lax.all_gather(kernel_slices, 'vel', axis=2, tiled=True)]
    all_to_all x0 -> x1, blocking collectives: none -> 31.9 us  [local(): full_slices = jnp.concatenate(lax.all_to_all(sent, 'vel', 0, 0), axis=2)]
    ppermute x2, waiting for transfers between devices: 0.01 us -> 5.59 us  [extended(): after = lax.ppermute(first, axis, down)]
    reshape x0 -> x1, local copies, waits for them, and re-layouts: none -> 3.93 us  [local(): full_slices = jnp.concatenate(lax.all_to_all(sent, 'vel', 0, 0), axis=2)]
  transfers between devices with their start and end apart: 8 -> 7, of which waited for: 6 -> 6; matrix products, arithmetic and copies ran while one was open for 2% -> 3% of each run, Pallas kernels for 0% -> 0%
where the time goes in v1:
time: 357 us; the launch traced here: 356 us
  waiting for transfers between devices  215 us (60%)
  matrix products  50.7 us (14%)
  blocking collectives  31.9 us (9%)
  starting transfers between devices  21.3 us (6%)
  local copies, waits for them, and re-layouts  18.4 us (5%)
  between operations  14.2 us (4%)
  other arithmetic  3.97 us (1%)
    all_gather x1, waiting for transfers between devices, local(): lax.all_gather(full_slices, 'space', axis=0, tiled=True)  133 us
    dot_general x16, matrix products, one_slice(): lax.dot_general(matrix, source, (((0,), (0,)), ((), ())), preferred_eleme...  50.7 us
    ppermute x2, waiting for transfers between devices, extended(): before = lax.ppermute(last, axis, up)  36.6 us
    all_to_all x1, blocking collectives, local(): full_slices = jnp.concatenate(lax.all_to_all(sent, 'vel', 0, 0), axis=2)  31.9 us
    all_to_all x1, waiting for transfers between devices, local(): lax.all_to_all(summed, 'vel', split_axis=0, concat_axis=1, tiled=True)  29.2 us
    all_to_all x1, waiting for transfers between devices, local(): lax.all_to_all(flattened, 'vel', split_axis=1, concat_axis=0, tiled=True)  10.1 us
    ppermute x2, starting transfers between devices, extended(): before = lax.ppermute(last, axis, up)  8.88 us
    unnamed x13, local copies, waits for them, and re-layouts  7.28 us
  transfers between devices with their start and end apart: 7, of which 6 were waited for; matrix products, arithmetic and copies ran while one was open for 3% of the time, Pallas kernels for 0%

profile of v1, /device:TPU:1, one launch (start us, length us, event | category | flops | bytes accessed | tf_op | source)
XLA Modules:
  0.0 356.0 jit_solution(5108275356762077209)
XLA Ops:
  7.2 0.0 all-gather.2.cloned.1.call-start
  7.2 1.2 stack.2
  8.4 31.9 %all_to_all.40 = bf16[8,1,1024,128]{3,2,1,0:T(8,128)(2,1)S(1)} all-to-all(bf16[8,1,1024,128]{3,2,1,0:T(8,128)(2,1)S(1)} %stack.2), channel_id=1, replica_groups=mesh['vel'=8,'space'=16] {'vel'}, dimensions={0} | all-to-all | bytes 4194304 | tf_op jit(solution)/shard_map/all_to_all | solution.py:66
  40.3 2.6 copy.18
  42.9 3.9 %copy.19 = bf16[1,1024,1024]{2,1,0:T(8,128)(2,1)} copy(bf16[1,1024,1024]{1,2,0:T(8,128)(2,1)} %bitcast.25) | data formatting | bytes 4194304 | tf_op jit(solution)/shard_map/reshape | solution.py:66
  46.8 0.0 all-gather.2.cloned.1.call-update
  46.9 2.0 copy.16
  48.9 0.0 copy-start.4
  48.9 0.0 copy-start.2
  48.9 0.1 fusion.18
  49.0 7.0 %collective-permute-start = (f32[128,1,8,128]{0,3,2,1:T(8,128)S(1)}, f32[128,1,8,128]{0,3,2,1:T(8,128)S(1)}, u32[]{:S(2)}, u32[]{:S(2)}) collective-permute-start(f32[128,1,8,128]{0,3,2,1:T(8,128)S(1)} %get-tuple-element.111), channel_id=1, source_target_pairs={{0,1},{1,2},{2,3},{3,4},{4,5},{5,6},{6,7},{7,8},{8,9},{9,10},{10,1... | collective-permute-start | bytes 1572872 | tf_op jit(solution)/shard_map/ppermute | solution.py:17
  56.0 1.9 collective-permute-start.1
  57.9 10.5 %collective-permute-done = f32[128,1,8,128]{0,3,2,1:T(8,128)S(1)} collective-permute-done((f32[128,1,8,128]{0,3,2,1:T(8,128)S(1)}, f32[128,1,8,128]{0,3,2,1:T(8,128)S(1)}, u32[]{:S(2)}, u32[]{:S(2)}) %collective-permute-start) | collective-permute-done | bytes 524320 | tf_op jit(solution)/shard_map/ppermute | solution.py:17
  68.4 5.6 %collective-permute-done.1 = f32[128,1,8,128]{0,3,2,1:T(8,128)S(1)} collective-permute-done((f32[128,1,8,128]{0,3,2,1:T(8,128)S(1)}, f32[128,1,8,128]{0,3,2,1:T(8,128)S(1)}, u32[]{:S(2)}, u32[]{:S(2)}) %collective-permute-start.1) | collective-permute-done | bytes 524320 | tf_op jit(solution)/shard_map/ppermute | solution.py:18
  74.0 1.9 multiply_add_fusion
  75.9 0.0 copy-start.3
  75.9 0.1 fusion.17
  76.0 1.9 collective-permute-start.2
  77.9 2.4 collective-permute-start.3
  80.4 26.1 %collective-permute-done.2 = f32[128,1,8,128]{0,3,2,1:T(8,128)S(1)} collective-permute-done((f32[128,1,8,128]{0,3,2,1:T(8,128)S(1)}, f32[128,1,8,128]{0,3,2,1:T(8,128)S(1)}, u32[]{:S(2)}, u32[]{:S(2)}) %collective-permute-start.2) | collective-permute-done | bytes 524320 | tf_op jit(solution)/shard_map/ppermute | solution.py:17
  106.5 1.9 fusion.15
  108.4 1.3 copy.17
  109.7 3.6 all-to-all-start
  113.3 10.1 %all-to-all-done = bf16[128,8,512]{2,0,1:T(8,128)(2,1)S(1)} async-done(((bf16[128,8,512]{2,0,1:T(8,128)(2,1)}), bf16[128,8,512]{2,0,1:T(8,128)(2,1)S(1)}, u32[]{:S(2)}, u32[]{:S(2)}) %all-to-all-start) | async-done | bytes 1048608 | tf_op jit(solution)/shard_map/all_to_all | solution.py:64
  123.5 133.4 %all-gather.2.cloned.1.call-done = bf16[16,1024,1024]{2,1,0:T(8,128)(2,1)} async-done(((bf16[1,1024,1024]{2,1,0:T(8,128)(2,1)}), bf16[16,1024,1024]{2,1,0:T(8,128)(2,1)}) %all-gather.2.cloned.1.call-update) | async-done | bytes 33554448 | tf_op jit(solution)/shard_map/all_gather | solution.py:68
  256.9 51.4 %while.14 = (s32[]{:T(128)}, f32[1024,512]{1,0:T(8,128)S(1)}, bf16[1024,512]{1,0:T(8,128)(2,1)S(1)}, bf16[16,1024,1024]{2,1,0:T(8,128)(2,1)}, s32[]{:T(128)}, /*index=5*/s32[]{:T(128)}, s32[]{:T(128)}, s32[]{:T(128)}) while((s32[]{:T(128)}, f32[1024,512]{1,0:T(8,128)S(1)}, bf16[1024,512]{1,0:T(8,128)(2,1)S(1)}, ...), condition=%wide.region_1.2_spmd.clone, body=%wide.region_0.1_spmd.clone.sunk | while | flops 1075315200 | bytes 7345809 | solution.py:49
  256.9 3.2 select_add_fusion.2
  260.1 3.2 select_add_fusion.2
  263.3 3.2 select_add_fusion.2
  266.5 3.2 select_add_fusion.2
  269.7 3.2 select_add_fusion.2
  273.0 3.2 select_add_fusion.2
  276.2 3.2 select_add_fusion.2
  279.4 3.2 select_add_fusion.2
  282.6 3.2 select_add_fusion.2
  285.8 3.2 select_add_fusion.2
  289.0 3.2 select_add_fusion.2
  292.3 3.2 select_add_fusion.2
  295.5 3.2 select_add_fusion.2
  298.7 3.2 select_add_fusion.2
  301.9 3.2 select_add_fusion.2
  305.1 3.2 select_add_fusion.2
  308.3 1.3 copy-done.1
  309.6 4.5 %all-to-all-start.2 = ((f32[8,128,512]{2,1,0:T(8,128)}), f32[8,128,512]{2,1,0:T(8,128)}, u32[]{:S(2)}, u32[]{:S(2)}) async-start(f32[8,128,512]{2,1,0:T(8,128)} %bitcast.28), calls=%async_computation.2 | async-start | bytes 4194304 | tf_op jit(solution)/shard_map/all_to_all | solution.py:69
  314.1 2.0 copy.21
  316.1 29.2 %all-to-all-done.2 = f32[8,128,512]{2,1,0:T(8,128)} async-done(((f32[8,128,512]{2,1,0:T(8,128)}), f32[8,128,512]{2,1,0:T(8,128)}, u32[]{:S(2)}, u32[]{:S(2)}) %all-to-all-start.2) | async-done | bytes 2097184 | tf_op jit(solution)/shard_map/all_to_all | solution.py:69
  345.3 1.9 copy.20
  347.2 2.0 copy.22
  (27 shorter events, 0.2 us)
Async XLA Ops:
  7.2 249.7 %all-gather.2.cloned.1.call-start = ((), (), s32[]{:S(2)}) async-start(), calls=%async_computation.3 | async-start | bytes 35651584 | tf_op jit(solution)/shard_map/all_gather | solution.py:68
  48.9 9.0 %copy-start.4 = (s32[128]{0:T(128)S(1)}, s32[128]{0:T(128)}, u32[]{:S(2)}) copy-start(s32[128]{0:T(128)} %param.9) | copy-start | bytes 1540
  48.9 9.0 %copy-start.2 = (s32[4,8,128]{2,1,0:T(8,128)S(1)}, s32[4,8,128]{2,1,0:T(8,128)}, u32[]{:S(2)}) copy-start(s32[4,8,128]{2,1,0:T(8,128)} %param.8) | copy-start | bytes 49156
  49.0 19.4 %collective-permute-start = (f32[128,1,8,128]{0,3,2,1:T(8,128)S(1)}, f32[128,1,8,128]{0,3,2,1:T(8,128)S(1)}, u32[]{:S(2)}, u32[]{:S(2)}) collective-permute-start(f32[128,1,8,128]{0,3,2,1:T(8,128)S(1)} %get-tuple-element.111), channel_id=1, source_target_pairs={{0,1},{1,2},{2,3},{3,4},{4,5},{5,6},{6,7},{7,8},{8,9},{9,10},{10,1... | collective-permute-start | bytes 1572872 | tf_op jit(solution)/shard_map/ppermute | solution.py:17
  56.0 18.1 %collective-permute-start.1 = (f32[128,1,8,128]{0,3,2,1:T(8,128)S(1)}, f32[128,1,8,128]{0,3,2,1:T(8,128)S(1)}, u32[]{:S(2)}, u32[]{:S(2)}) collective-permute-start(f32[128,1,8,128]{0,3,2,1:T(8,128)S(1)} %get-tuple-element.112), channel_id=1, source_target_pairs={{1,0},{2,1},{3,2},{4,3},{5,4},{6,5},{7,6},{8,7},{9,8},{10,9},{11,1... | collective-permute-start | bytes 1572872 | tf_op jit(solution)/shard_map/ppermute | solution.py:18
  75.9 30.6 %copy-start.3 = (f32[128]{0:T(128)S(1)}, f32[128]{0:T(128)}, u32[]{:S(2)}) copy-start(f32[128]{0:T(128)} %param.10) | copy-start | bytes 1540
  76.0 30.5 %collective-permute-start.2 = (f32[128,1,8,128]{0,3,2,1:T(8,128)S(1)}, f32[128,1,8,128]{0,3,2,1:T(8,128)S(1)}, u32[]{:S(2)}, u32[]{:S(2)}) collective-permute-start(f32[128,1,8,128]{0,3,2,1:T(8,128)S(1)} %get-tuple-element.109), channel_id=1, source_target_pairs={{0,1},{1,2},{2,3},{3,4},{4,5},{5,6},{6,7},{7,8},{8,9},{9,10},{10,1... | collective-permute-start | bytes 1572872 | tf_op jit(solution)/shard_map/ppermute | solution.py:17
  77.9 28.5 %collective-permute-start.3 = (f32[128,1,8,128]{0,3,2,1:T(8,128)S(1)}, f32[128,1,8,128]{0,3,2,1:T(8,128)S(1)}, u32[]{:S(2)}, u32[]{:S(2)}) collective-permute-start(f32[128,1,8,128]{0,3,2,1:T(8,128)S(1)} %get-tuple-element.110), channel_id=1, source_target_pairs={{1,0},{2,1},{3,2},{4,3},{5,4},{6,5},{7,6},{8,7},{9,8},{10,9},{11,1... | collective-permute-start | bytes 1572872 | tf_op jit(solution)/shard_map/ppermute | solution.py:18
  109.7 13.7 %all-to-all-start = ((bf16[128,8,512]{2,0,1:T(8,128)(2,1)}), bf16[128,8,512]{2,0,1:T(8,128)(2,1)S(1)}, u32[]{:S(2)}, u32[]{:S(2)}) async-start(bf16[128,8,512]{2,0,1:T(8,128)(2,1)} %copy.17), calls=%async_computation | async-start | bytes 2097152 | tf_op jit(solution)/shard_map/all_to_all | solution.py:64
  308.3 1.3 copy-start.1
  309.6 4.5 %copy-start = (f32[128,4,8,128]{0,3,2,1:T(8,128)S(1)}, f32[128,4,8,128]{0,3,2,1:T(8,128)}, u32[]{:S(2)}) copy-start(f32[128,4,8,128]{0,3,2,1:T(8,128)} %get-tuple-element.108) | copy-start | bytes 6291460
  309.6 35.7 %all-to-all-start.2 = ((f32[8,128,512]{2,1,0:T(8,128)}), f32[8,128,512]{2,1,0:T(8,128)}, u32[]{:S(2)}, u32[]{:S(2)}) async-start(f32[8,128,512]{2,1,0:T(8,128)} %bitcast.28), calls=%async_computation.2 | async-start | bytes 4194304 | tf_op jit(solution)/shard_map/all_to_all | solution.py:69
Sparse Core Ops, SparseCore 0:
  47.0 209.8 all-gather.1
